TPU v7x, 32 devices: a whole 2x2x4 slice. The times are simulated.
32 devices in a mesh: grp: 2 (over x), seq: 8 (over z, y), col: 2 (over core).
Axes of the slice: x: 2, y: 2, z: 4, core: 2. Of those that a mesh axis runs over, the one named last changes fastest.
Arguments:
- signal: bfloat16 [8192, 1408], P(('grp', 'seq'), 'col'), parts along dimension 0, may hold values from -6 to 6
- conv_weight: bfloat16 [5, 1408, 1408], P(None, None, 'col'), may hold values from -0.15625 to 0.15625
- conv_gain: float32 [1408], replicated, may hold values from 0.1 to 1.9
- embed_weight: bfloat16 [1408, 1536], P('col', 'seq'), may hold values from -0.15625 to 0.15625
- attn_gain: float32 [1536], replicated, may hold values from 0.1 to 1.9
- query_weight: bfloat16 [1536, 1024], P('seq'), may hold values from -4 to 4
- keyvalue_weight: bfloat16 [1536, 320], P('seq'), may hold values from -4 to 4
- output_weight: bfloat16 [1536, 1536], P(None, 'seq'), may hold values from -0.15625 to 0.15625
- rowcol_weight: bfloat16 [1536, 256], replicated, may hold values from -0.15625 to 0.15625
- pair_weight: bfloat16 [128, 128], replicated, may hold values from -0.5 to 0.5
Outputs:
- tokens: bfloat16 [2048, 1536], P(('grp', 'seq', 'col')), parts along dimension 0
- pair_out: bfloat16 [128, 64, 128], P(('grp', 'seq'), 'col'), parts along dimension 0
There are 2 independent parts, one for each index of `grp`. A program takes and returns all parts, laid end to end along the dimension named above; an argument that names none is the same for every part. Nothing has to cross between parts.
All inputs are finite; a program needn't handle non-finite values.
Results may differ from a plain program's by a relative error of at most 0.015.
Values may be sent and summed in bfloat16 or wider, within the bound.
A program may use at most 128 MiB of HBM per device.

v0:
```python
import jax
import jax.numpy as jnp
from jax import lax
from jax.sharding import PartitionSpec as P

DK = 128
DV = 192
POOL = 4
PAIR_POOL = 16


def with_halo(array, sides, width):
    for axis, dim in sides:
        size, length = (lax.axis_size(axis), array.shape[dim])
        up = [(i, (i + 1) % size) for i in range(size - 1)]
        down = [(j, i) for i, j in up]
        last = lax.slice_in_dim(array, length - width, length, axis=dim)
        first = lax.slice_in_dim(array, 0, width, axis=dim)
        before = lax.ppermute(last, axis, up)
        after = lax.ppermute(first, axis, down)
        array = jnp.concatenate([before, array, after], axis=dim)
    return array


def rms_scale(values, gain_vector):
    return (
        values * lax.rsqrt(jnp.mean(values * values, axis=-1, keepdims=True) + 1e-06) * gain_vector
    )


def attention_parts(queries, head_count):
    query_rows = queries.reshape(queries.shape[0] * head_count, DK)

    def absorb(running, pieces, first_row):
        running_max, running_sum, accumulated = running
        key_piece, value_piece = pieces
        scores = lax.dot_general(
            query_rows, key_piece, (((1,), (1,)), ((), ())), preferred_element_type=jnp.float32
        )
        newest_max = jnp.maximum(running_max, jnp.max(scores, axis=1))
        weights = jnp.exp(scores - newest_max[:, None])
        running_sum = jnp.sum(weights, axis=1)
        accumulated = jnp.dot(
            weights.astype(jnp.bfloat16), value_piece, preferred_element_type=jnp.float32
        )
        return (newest_max, running_sum, accumulated)

    row_count = query_rows.shape[0]
    initial = (
        jnp.full((row_count,), -1e30, jnp.float32),
        jnp.zeros((row_count,), jnp.float32),
        jnp.zeros((row_count, DV), jnp.float32),
    )
    return (absorb, initial)


def finish_attention(result, token_count):
    running_max, running_sum, accumulated = result
    return (accumulated / running_sum[:, None]).astype(jnp.bfloat16).reshape(token_count, -1)


def on_device(
    signal,
    conv_weight,
    conv_gain,
    embed_weight,
    attn_gain,
    query_weight,
    keyvalue_weight,
    output_weight,
    rowcol_weight,
    pair_weight,
):
    positions = signal.shape[0]
    tap_count = conv_weight.shape[0]
    halo_width = tap_count // 2
    padded = with_halo(signal, (("seq", 0),), halo_width)
    widened = lax.all_gather(padded, "col", axis=1, tiled=True)
    activated = jax.nn.gelu(
        rms_scale(widened.astype(jnp.float32), conv_gain), approximate=True
    ).astype(jnp.bfloat16)
    summed = signal.astype(jnp.float32)
    for tap_index in range(tap_count):
        summed = summed + jnp.dot(
            activated[tap_index : tap_index + positions],
            conv_weight[tap_index],
            preferred_element_type=jnp.float32,
        )
    pooled = jnp.mean(summed.reshape(positions // POOL, POOL, -1), axis=1).astype(jnp.bfloat16)
    embed_full = lax.all_gather(embed_weight, "seq", axis=1, tiled=True)
    col_count = lax.axis_size("col")
    embedded = lax.psum_scatter(
        jnp.dot(pooled, embed_full, preferred_element_type=jnp.float32).astype(jnp.bfloat16),
        "col",
        scatter_dimension=0,
        tiled=True,
    )
    normed = rms_scale(embedded.astype(jnp.float32), attn_gain).astype(jnp.bfloat16)
    head_count = query_weight.shape[1] // DK
    scaling = DK ** (-0.5)
    col_index = lax.axis_index("col")
    local_heads = head_count // col_count
    group_tokens = lax.all_gather(normed, "col", axis=0, tiled=True)
    group_count = group_tokens.shape[0]
    query_half = lax.dynamic_slice_in_dim(
        query_weight, col_index * local_heads * DK, local_heads * DK, 1
    )
    query_sum = jnp.dot(
        group_tokens,
        lax.all_gather(query_half, "seq", axis=0, tiled=True),
        preferred_element_type=jnp.float32,
    )
    keyvalue_sum = jnp.dot(
        group_tokens,
        lax.all_gather(keyvalue_weight, "seq", axis=0, tiled=True),
        preferred_element_type=jnp.float32,
    )
    queries = (query_sum * scaling).astype(jnp.bfloat16)
    keyvalue = keyvalue_sum.astype(jnp.bfloat16)
    absorb, initial = attention_parts(queries, local_heads)
    result = absorb(
        initial,
        (
            lax.all_gather(keyvalue[:, :DK], "seq", axis=0, tiled=True),
            lax.all_gather(keyvalue[:, DK:], "seq", axis=0, tiled=True),
        ),
        jnp.int32(0),
    )
    attended = finish_attention(result, group_count)
    output_half = lax.dynamic_slice_in_dim(
        output_weight, col_index * local_heads * DV, local_heads * DV, 0
    )
    partial_out = jnp.dot(
        attended,
        lax.all_gather(output_half, "seq", axis=1, tiled=True),
        preferred_element_type=jnp.float32,
    )
    attention_out = lax.psum_scatter(
        partial_out.astype(jnp.bfloat16), "col", scatter_dimension=0, tiled=True
    ).astype(jnp.float32)
    tokens = (embedded.astype(jnp.float32) + attention_out).astype(jnp.bfloat16)
    pair_pool = jnp.mean(
        tokens.astype(jnp.float32).reshape(-1, PAIR_POOL, tokens.shape[1]), axis=1
    ).astype(jnp.bfloat16)
    projected = jnp.dot(pair_pool, rowcol_weight, preferred_element_type=jnp.float32).astype(
        jnp.bfloat16
    )
    features = pair_weight.shape[0]
    row_block = lax.all_gather(projected, "col", axis=0, tiled=True)
    column_all = lax.all_gather(row_block[:, features:], "seq", axis=0, tiled=True)
    row_part = row_block[:, :features]
    column_span = column_all.shape[0] // col_count
    column_part = lax.dynamic_slice_in_dim(
        column_all, lax.axis_index("col") * column_span, column_span, 0
    )
    hidden = jax.nn.gelu(
        row_part.astype(jnp.float32)[:, None, :] + column_part.astype(jnp.float32)[None, :, :],
        approximate=True,
    ).astype(jnp.bfloat16)
    pair_out = jnp.dot(
        hidden.reshape(-1, features), pair_weight, preferred_element_type=jnp.float32
    ).astype(jnp.bfloat16)
    return (tokens, pair_out.reshape(row_part.shape[0], column_span, features))


def solution(mesh):
    placed = (
        P(("grp", "seq"), "col"),
        P(None, None, "col"),
        P(),
        P("col", "seq"),
        P(),
        P("seq", None),
        P("seq", None),
        P(None, "seq"),
        P(),
        P(),
    )
    return jax.shard_map(
        on_device,
        mesh=mesh,
        in_specs=placed,
        out_specs=(P(("grp", "seq", "col"), None), P(("grp", "seq"), "col", None)),
        check_vma=False,
    )
```

profile of v0, /device:TPU:0, one launch (start us, length us, event | category | flops | bytes accessed | tf_op | source)
XLA Modules:
  0.0 256.0 jit_solution(12248278608278916954)
XLA Ops:
  7.2 0.0 copy-start
  7.2 0.0 all-gather.13.cloned.1.call-start
  7.2 1.4 copy.19
  8.7 4.9 %collective-permute-start = (bf16[2,704]{1,0:T(2,128)(2,1)S(1)}, bf16[2,704]{1,0:T(2,128)(2,1)S(1)}, u32[]{:S(2)}, u32[]{:S(2)}) collective-permute-start(bf16[2,704]{1,0:T(2,128)(2,1)S(1)} %get-tuple-element.4), channel_id=1, source_target_pairs={{0,2},{2,4},{4,6},{6,8},{8,10},{10,12},{12,14},{1,3},{3,5},{5,7},{... | collective-permute-start | bytes 8456 | tf_op jit(solution)/shard_map/ppermute | solution.py:19
  13.6 1.3 collective-permute-start.1
  14.9 4.2 %collective-permute-done.1 = bf16[2,704]{1,0:T(2,128)(2,1)S(1)} collective-permute-done((bf16[2,704]{1,0:T(2,128)(2,1)S(1)}, bf16[2,704]{1,0:T(2,128)(2,1)S(1)}, u32[]{:S(2)}, u32[]{:S(2)}) %collective-permute-start.1) | collective-permute-done | bytes 2848 | tf_op jit(solution)/shard_map/ppermute | solution.py:20
  19.1 1.1 maximum_bitcast_fusion
  20.2 0.0 all-gather.13.cloned.1.call-update
  20.2 0.0 all-gather.7.cloned.1.call-start
  20.3 0.7 all-gather.7.cloned.1.call-update
  21.0 0.0 reduce-scatter.3.cloned.1.call-start
  21.0 10.3 %all-gather.13.cloned.1.call-done = bf16[2,704,516]{1,2,0:T(8,128)(2,1)} async-done(((bf16[1,704,516]{1,2,0:T(8,128)(2,1)}), bf16[2,704,516]{1,2,0:T(8,128)(2,1)}) %all-gather.13.cloned.1.call-update) | async-done | bytes 1453072 | tf_op jit(solution)/shard_map/all_gather | solution.py:78
  31.4 4.3 %copy.22 = f32[2,704,516]{1,0,2:T(2,128)} copy(bf16[2,704,516]{1,2,0:T(8,128)(2,1)} %all-gather.13.cloned.1.call-done) | data formatting | bytes 4359168 | tf_op jit(solution)/shard_map/convert_element_type | solution.py:80
  35.6 5.3 %reshape.62 = f32[1408,516]{0,1:T(8,128)} reshape(f32[2,704,516]{1,0,2:T(2,128)} %copy.22) | data formatting | bytes 5812224 | tf_op jit(solution)/shard_map/convert_element_type | solution.py:80
  41.0 2.4 multiply_reduce_fusion
  43.4 0.5 copy-done.1
  43.9 1.2 fusion.7
  45.1 0.0 copy-start.4
  45.1 3.0 %fusion.16 = f32[512,704]{0,1:T(8,128)S(1)} fusion(bf16[5,1408,704]{1,2,0:T(8,128)(2,1)} %param.11, bf16[516,1408]{1,0:T(8,128)(2,1)S(1)} %fusion.7), kind=kOutput, calls=%fused_computation.21 | convolution fusion | flops 1015021568 | bytes 4866048 | tf_op jit(solution)/shard_map/dot_general | solution.py:84
  48.1 1.4 copy-done.4
  49.6 1.3 fusion.12
  50.9 1.3 fusion.10
  52.2 0.0 copy-start.2
  52.2 1.3 fusion.8
  53.6 1.5 add_add_fusion
  55.1 1.6 copy.23
  56.7 1.8 reshape.50
  58.5 0.9 reduce_sum.46
  59.4 0.0 copy-start.6
  59.5 27.1 %all-gather.7.cloned.1.call-done = bf16[704,1536]{0,1:T(8,128)(2,1)} async-done(((bf16[704,192]{0,1:T(8,128)(2,1)}), bf16[704,1536]{0,1:T(8,128)(2,1)}) %all-gather.7.cloned.1.call-update) | async-done | bytes 2162704 | tf_op jit(solution)/shard_map/all_gather | solution.py:90
  86.6 3.3 %convolution_convert_fusion.1 = bf16[128,1536]{1,0:T(8,128)(2,1)} fusion(bf16[704,1536]{0,1:T(8,128)(2,1)} %all-gather.7.cloned.1.call-done, f32[128,704]{1,0:T(8,128)S(1)} %reduce_sum.46), kind=kOutput, calls=%fused_computation.11 | convolution fusion | flops 277200896 | bytes 2916352 | tf_op jit(solution)/shard_map/dot_general | solution.py:93
  89.9 0.0 reduce-scatter.3.cloned.1.call-update
  89.9 0.0 all-gather.9.cloned.1.call-start
  90.0 0.7 constant_dynamic-slice_fusion.1
  90.7 0.0 all-gather.9.cloned.1.call-update
  90.7 0.0 all-gather.11.cloned.1.call-start
  90.7 0.8 constant_dynamic-slice_fusion
  91.5 0.0 all-gather.11.cloned.1.call-update
  91.5 0.0 reduce-scatter.5.cloned.1.call-start
  91.6 34.7 %all_gather.34 = bf16[1536,320]{1,0:T(8,128)(2,1)S(1)} all-gather(bf16[192,320]{1,0:T(8,128)(2,1)S(1)} %copy-done.6), channel_id=1, replica_groups=mesh['grp'=2,'seq'=8,'col'=2] {'seq'}, dimensions={0}, use_global_device_ids=true | all-gather | bytes 1105920 | tf_op jit(solution)/shard_map/all_gather | solution.py:115
  126.3 1.1 fusion.39
  127.3 1.0 fusion.41
  128.4 2.3 all_gather.32
  130.7 0.5 convolution_convert_fusion.2
  131.2 17.2 %all-gather.9.cloned.1.call-done = bf16[1536,512]{1,0:T(8,128)(2,1)} async-done(((bf16[192,512]{1,0:T(8,128)(2,1)}), bf16[1536,512]{1,0:T(8,128)(2,1)}) %all-gather.9.cloned.1.call-update) | async-done | bytes 1572880 | tf_op jit(solution)/shard_map/all_gather | solution.py:110
  148.5 1.8 fusion.35
  150.3 0.1 reshape.51
  150.4 27.6 %all_gather.35 = bf16[1024,128]{0,1:T(8,128)(2,1)S(1)} all-gather(bf16[128,128]{0,1:T(8,128)(2,1)S(1)} %slice.71), channel_id=1, replica_groups=mesh['grp'=2,'seq'=8,'col'=2] {'seq'}, dimensions={0}, use_global_device_ids=true | all-gather | bytes 294912 | tf_op jit(solution)/shard_map/all_gather | solution.py:124
  177.9 29.5 %all_gather.36 = bf16[1024,192]{0,1:T(8,128)(2,1)S(1)} all-gather(bf16[128,192]{0,1:T(8,128)(2,1)S(1)} %slice.72), channel_id=1, replica_groups=mesh['grp'=2,'seq'=8,'col'=2] {'seq'}, dimensions={0}, use_global_device_ids=true | all-gather | bytes 442368 | tf_op jit(solution)/shard_map/all_gather | solution.py:125
  207.5 0.5 fusion.57
  208.0 0.5 fusion.23
  208.5 0.6 fusion.34
  209.1 0.1 copy.24
  209.2 0.3 reshape.52
  209.5 0.0 all-gather.11.cloned.1.call-done
  209.6 3.3 %convolution_convert_fusion = bf16[128,1536]{1,0:T(8,128)(2,1)} fusion(bf16[128,768]{1,0:T(8,128)(2,1)S(1)} %reshape.52, bf16[768,1536]{0,1:T(8,128)(2,1)} %all-gather.11.cloned.1.call-done), kind=kOutput, calls=%fused_computation.10 | convolution fusion | flops 302186496 | bytes 2949120 | tf_op jit(solution)/shard_map/dot_general | solution.py:133
  212.9 0.0 reduce-scatter.5.cloned.1.call-update
  212.9 5.2 %reduce-scatter.5.cloned.1.call-done = bf16[64,1536]{1,0:T(8,128)(2,1)} async-done(((bf16[128,1536]{1,0:T(8,128)(2,1)}), bf16[64,1536]{1,0:T(8,128)(2,1)}) %reduce-scatter.5.cloned.1.call-update) | async-done | bytes 196624 | tf_op jit(solution)/shard_map/reduce_scatter | solution.py:138
  218.1 1.7 convert_reduce_fusion
  219.8 0.2 fusion.36
  220.0 1.8 all-gather.1
  221.9 26.4 %all_gather.39 = bf16[64,128]{1,0:T(8,128)(2,1)S(1)} all-gather(bf16[8,128]{1,0:T(8,128)(2,1)S(1)} %get-tuple-element.7), channel_id=1, replica_groups=mesh['grp'=2,'seq'=8,'col'=2] {'seq'}, dimensions={0}, use_global_device_ids=true | all-gather | bytes 18432 | tf_op jit(solution)/shard_map/all_gather | solution.py:150
  248.3 0.1 fusion.51
  248.4 0.8 convolution_convert_fusion.3
  (28 shorter events, 0.1 us)
Async XLA Ops:
  7.2 212.6 %copy-start = (bf16[1536,256]{1,0:T(8,128)(2,1)S(1)}, bf16[1536,256]{1,0:T(8,128)(2,1)}, u32[]{:S(2)}) copy-start(bf16[1536,256]{1,0:T(8,128)(2,1)} %param.18) | copy-start | bytes 2359300
  7.2 24.2 %all-gather.13.cloned.1.call-start = ((), (), s32[]{:S(2)}) async-start(), calls=%async_computation.7 | async-start | bytes 2396160 | tf_op jit(solution)/shard_map/all_gather | solution.py:78
  8.7 6.2 %collective-permute-start = (bf16[2,704]{1,0:T(2,128)(2,1)S(1)}, bf16[2,704]{1,0:T(2,128)(2,1)S(1)}, u32[]{:S(2)}, u32[]{:S(2)}) collective-permute-start(bf16[2,704]{1,0:T(2,128)(2,1)S(1)} %get-tuple-element.4), channel_id=1, source_target_pairs={{0,2},{2,4},{4,6},{6,8},{8,10},{10,12},{12,14},{1,3},{3,5},{5,7},{... | collective-permute-start | bytes 8456 | tf_op jit(solution)/shard_map/ppermute | solution.py:19
  13.6 5.5 %collective-permute-start.1 = (bf16[2,704]{1,0:T(2,128)(2,1)S(1)}, bf16[2,704]{1,0:T(2,128)(2,1)S(1)}, u32[]{:S(2)}, u32[]{:S(2)}) collective-permute-start(bf16[2,704]{1,0:T(2,128)(2,1)S(1)} %get-tuple-element.5), channel_id=1, source_target_pairs={{2,0},{4,2},{6,4},{8,6},{10,8},{12,10},{14,12},{3,1},{5,3},{7,5},{... | collective-permute-start | bytes 8456 | tf_op jit(solution)/shard_map/ppermute | solution.py:20
  20.2 66.3 %all-gather.7.cloned.1.call-start = ((), (), s32[]{:S(2)}) async-start(), calls=%async_computation.2 | async-start | bytes 2654208 | tf_op jit(solution)/shard_map/all_gather | solution.py:90
  21.0 105.3 %reduce-scatter.3.cloned.1.call-start = ((), (), s32[]{:S(2)}) async-start(), calls=%async_computation.3 | async-start | bytes 589824 | tf_op jit(solution)/shard_map/reduce_scatter | solution.py:92
  41.0 2.9 %copy-start.1 = (f32[1408,516]{0,1:T(8,128)S(1)}, f32[1408,516]{0,1:T(8,128)}, u32[]{:S(2)}) copy-start(f32[1408,516]{0,1:T(8,128)} %reshape.62) | copy-start | bytes 8718340
  41.0 2.9 %copy-start.9 = (f32[1408]{0:T(1024)S(1)}, f32[1408]{0:T(1024)}, u32[]{:S(2)}) copy-start(f32[1408]{0:T(1024)} %param.12) | copy-start | bytes 16900
  45.1 4.4 %copy-start.4 = (bf16[5,1408,704]{1,2,0:T(8,128)(2,1)S(1)}, bf16[5,1408,704]{1,2,0:T(8,128)(2,1)}, u32[]{:S(2)}) copy-start(bf16[5,1408,704]{1,2,0:T(8,128)(2,1)} %param.11) | copy-start | bytes 29736964
  52.2 1.4 copy-start.2
  59.4 30.5 %copy-start.7 = (bf16[192,1024]{1,0:T(8,128)(2,1)S(1)}, bf16[192,1024]{1,0:T(8,128)(2,1)}, u32[]{:S(2)}) copy-start(bf16[192,1024]{1,0:T(8,128)(2,1)} %param.15) | copy-start | bytes 1179652
  59.4 31.3 %copy-start.5 = (bf16[1536,192]{0,1:T(8,128)(2,1)S(1)}, bf16[1536,192]{0,1:T(8,128)(2,1)}, u32[]{:S(2)}) copy-start(bf16[1536,192]{0,1:T(8,128)(2,1)} %param.17) | copy-start | bytes 1769476
  59.4 32.1 %copy-start.6 = (bf16[192,320]{1,0:T(8,128)(2,1)S(1)}, bf16[192,320]{1,0:T(8,128)(2,1)}, u32[]{:S(2)}) copy-start(bf16[192,320]{1,0:T(8,128)(2,1)} %param.16) | copy-start | bytes 368644
  89.9 37.5 %copy-start.10 = (f32[1536]{0:T(1024)S(1)}, f32[1536]{0:T(1024)}, u32[]{:S(2)}) copy-start(f32[1536]{0:T(1024)} %param.14) | copy-start | bytes 18436
  89.9 58.6 %all-gather.9.cloned.1.call-start = ((), (), s32[]{:S(2)}) async-start(), calls=%async_computation.4 | async-start | bytes 1769472 | tf_op jit(solution)/shard_map/all_gather | solution.py:110
  90.7 118.9 %all-gather.11.cloned.1.call-start = ((), (), s32[]{:S(2)}) async-start(), calls=%async_computation.5 | async-start | bytes 2654208 | tf_op jit(solution)/shard_map/all_gather | solution.py:135
  91.5 126.6 %reduce-scatter.5.cloned.1.call-start = ((), (), s32[]{:S(2)}) async-start(), calls=%async_computation.6 | async-start | bytes 589824 | tf_op jit(solution)/shard_map/reduce_scatter | solution.py:138
  209.2 8.9 %copy-start.3 = (bf16[64,1536]{1,0:T(8,128)(2,1)S(1)}, bf16[64,1536]{1,0:T(8,128)(2,1)}, u32[]{:S(2)}) copy-start(bf16[64,1536]{1,0:T(8,128)(2,1)} %reduce-scatter.3.cloned.1.call-done) | copy-start | bytes 589828
  209.5 38.8 %copy-start.8 = (bf16[128,128]{1,0:T(8,128)(2,1)S(1)}, bf16[128,128]{1,0:T(8,128)(2,1)}, u32[]{:S(2)}) copy-start(bf16[128,128]{1,0:T(8,128)(2,1)} %param.19) | copy-start | bytes 98308
Sparse Core Ops, SparseCore 0:
  20.3 10.9 all-gather.12
  33.5 52.9 all-gather.6
  90.0 6.3 reduce-scatter.2
  99.0 49.4 all-gather.8
  150.5 55.1 all-gather.10
  213.0 5.0 reduce-scatter.4
where the time goes:
time: 257 us; the launch traced here: 256 us
  blocking collectives  122 us (47%)
  waiting for transfers between devices  64.9 us (25%)
  matrix products  19.5 us (8%)
  local copies, waits for them, and re-layouts  18.4 us (7%)
  between operations  14.4 us (6%)
  other arithmetic  10.1 us (4%)
  starting transfers between devices  6.43 us (3%)
    all_gather x1, blocking collectives, on_device(): lax.all_gather(keyvalue_weight, 'seq', axis=0, tiled=True)  34.7 us
    all_gather x1, blocking collectives, on_device(): lax.all_gather(keyvalue[:, DK:], 'seq', axis=0, tiled=True)  29.5 us
    all_gather x1, blocking collectives, on_device(): lax.all_gather(keyvalue[:, :DK], 'seq', axis=0, tiled=True)  27.6 us
    all_gather x1, waiting for transfers between devices, on_device(): embed_full = lax.all_gather(embed_weight, 'seq', axis=1, tiled=True)  27.1 us
    all_gather x1, blocking collectives, on_device(): lax.all_gather(row_block[:, features:], 'seq', axis=0, tiled=True)  26.4 us
    all_gather x1, waiting for transfers between devices, on_device(): lax.all_gather(query_half, 'seq', axis=0, tiled=True)  17.2 us
    all_gather x1, waiting for transfers between devices, on_device(): widened = lax.all_gather(padded, 'col', axis=1, tiled=True)  10.3 us
    convert_element_type x2, local copies, waits for them, and re-layouts, on_device(): widened.astype(jnp.float32)  9.6 us
  transfers between devices with their start and end apart: 8, of which 5 were waited for; matrix products, arithmetic and copies ran while one was open for 13% of the time, Pallas kernels for 0%

commit v1 on v0

--- a/solution.py
+++ b/solution.py
@@ -7,6 +7,28 @@
 DV = 192
 POOL = 4
 PAIR_POOL = 16
+
+
+def in_order(blocks, dim):
+    shape = list(blocks.shape[1:])
+    shape[dim] *= blocks.shape[0]
+    return jnp.moveaxis(blocks, 0, dim).reshape(shape)
+
+
+def grow_blocks(x, axis):
+    size = lax.axis_size(axis)
+    tiles = x[None]
+    for level in range(size.bit_length() - 1):
+        bit = 1 << level
+        other = lax.ppermute(tiles, axis, [(i, i ^ bit) for i in range(size)])
+        both = jnp.stack([tiles, other])
+        upper = lax.axis_index(axis) >> level & 1
+        tiles = jnp.where(upper == 0, both, both[::-1]).reshape(-1, *x.shape)
+    return tiles
+
+
+def collect(x, axis, dim):
+    return in_order(grow_blocks(x, axis), dim)
 
 
 def with_halo(array, sides, width):
@@ -106,9 +128,7 @@
         query_weight, col_index * local_heads * DK, local_heads * DK, 1
     )
     query_sum = jnp.dot(
-        group_tokens,
-        lax.all_gather(query_half, "seq", axis=0, tiled=True),
-        preferred_element_type=jnp.float32,
+        group_tokens, collect(query_half, "seq", 0), preferred_element_type=jnp.float32
     )
     keyvalue_sum = jnp.dot(
         group_tokens,

time: 257 us -> 283 us (1.10)
  blocking collectives: 122 us -> 157 us
  waiting for transfers between devices: 64.9 us -> 52.2 us
  starting transfers between devices: 6.43 us -> 13.1 us
    all_gather x1, blocking collectives: 34.7 us -> 72.1 us  [on_device(): lax.all_gather(keyvalue_weight, 'seq', axis=0, tiled=True)]
    all_gather x1 -> x0, waiting for transfers between devices: 17.2 us -> none  [on_device(): lax.all_gather(query_half, 'seq', axis=0, tiled=True)]
    ppermute x0 -> x3, waiting for transfers between devices: none -> 7.17 us  [grow_blocks(): other = lax.ppermute(tiles, axis, [(i, i ^ bit) for i in range(size)])]
    ppermute x0 -> x3, starting transfers between devices: none -> 6.61 us  [grow_blocks(): other = lax.ppermute(tiles, axis, [(i, i ^ bit) for i in range(size)])]
  transfers between devices with their start and end apart: 8 -> 10, of which waited for: 5 -> 5; matrix products, arithmetic and copies ran while one was open for 13% -> 13% of each run, Pallas kernels for 0% -> 0%
where the time goes in v1:
time: 283 us
  blocking collectives  157 us (55%)
  waiting for transfers between devices  52.2 us (18%)
  matrix products  18.2 us (6%)
  local copies, waits for them, and re-layouts  17.7 us (6%)
  between operations  14.1 us (5%)
  starting transfers between devices  13.1 us (5%)
  other arithmetic  10.9 us (4%)
    all_gather x1, blocking collectives, on_device(): lax.all_gather(keyvalue_weight, 'seq', axis=0, tiled=True)  72.1 us
    all_gather x1, blocking collectives, on_device(): lax.all_gather(keyvalue[:, DK:], 'seq', axis=0, tiled=True)  27.3 us
    all_gather x1, waiting for transfers between devices, on_device(): embed_full = lax.all_gather(embed_weight, 'seq', axis=1, tiled=True)  27.1 us
    all_gather x1, blocking collectives, on_device(): lax.all_gather(keyvalue[:, :DK], 'seq', axis=0, tiled=True)  26.8 us
    all_gather x1, blocking collectives, on_device(): lax.all_gather(row_block[:, features:], 'seq', axis=0, tiled=True)  26.4 us
    convert_element_type x2, local copies, waits for them, and re-layouts, on_device(): widened.astype(jnp.float32)  9.61 us
    dot_general x5, matrix products, on_device(): jnp.dot(activated[tap_index:tap_index + positions], conv_weight[tap_index...  8.49 us
    all_gather x1, waiting for transfers between devices, on_device(): widened = lax.all_gather(padded, 'col', axis=1, tiled=True)  7.79 us
  transfers between devices with their start and end apart: 10, of which 5 were waited for; matrix products, arithmetic and copies ran while one was open for 13% of the time, Pallas kernels for 0%

profile of v1, /device:TPU:0, one launch (start us, length us, event | category | flops | bytes accessed | tf_op | source)
XLA Modules:
  0.0 282.8 jit_solution(16774767881286605527)
XLA Ops:
  7.2 0.0 all-gather.10.cloned.1.call-start
  7.2 1.4 copy.19
  8.7 5.0 %collective-permute-start = (bf16[2,704]{1,0:T(2,128)(2,1)S(1)}, bf16[2,704]{1,0:T(2,128)(2,1)S(1)}, u32[]{:S(2)}, u32[]{:S(2)}) collective-permute-start(bf16[2,704]{1,0:T(2,128)(2,1)S(1)} %get-tuple-element.4), channel_id=1, source_target_pairs={{0,2},{2,4},{4,6},{6,8},{8,10},{10,12},{12,14},{1,3},{3,5},{5,7},{... | collective-permute-start | bytes 8456 | tf_op jit(solution)/shard_map/ppermute | solution.py:41
  13.7 1.3 collective-permute-start.1
  15.1 4.2 %collective-permute-done.1 = bf16[2,704]{1,0:T(2,128)(2,1)S(1)} collective-permute-done((bf16[2,704]{1,0:T(2,128)(2,1)S(1)}, bf16[2,704]{1,0:T(2,128)(2,1)S(1)}, u32[]{:S(2)}, u32[]{:S(2)}) %collective-permute-start.1) | collective-permute-done | bytes 2848 | tf_op jit(solution)/shard_map/ppermute | solution.py:42
  19.2 1.1 maximum_bitcast_fusion
  20.3 0.0 all-gather.10.cloned.1.call-update
  20.4 0.0 all-gather.6.cloned.1.call-start
  20.4 0.7 all-gather.6.cloned.1.call-update
  21.1 0.0 reduce-scatter.3.cloned.1.call-start
  21.2 2.5 collective-permute-start.2
  23.7 7.8 %all-gather.10.cloned.1.call-done = bf16[2,704,516]{1,2,0:T(8,128)(2,1)} async-done(((bf16[1,704,516]{1,2,0:T(8,128)(2,1)}), bf16[2,704,516]{1,2,0:T(8,128)(2,1)}) %all-gather.10.cloned.1.call-update) | async-done | bytes 1453072 | tf_op jit(solution)/shard_map/all_gather | solution.py:100
  31.5 4.3 %copy.22 = f32[2,704,516]{1,0,2:T(2,128)} copy(bf16[2,704,516]{1,2,0:T(8,128)(2,1)} %all-gather.10.cloned.1.call-done) | data formatting | bytes 4359168 | tf_op jit(solution)/shard_map/convert_element_type | solution.py:102
  35.8 5.3 %reshape.70 = f32[1408,516]{0,1:T(8,128)} reshape(f32[2,704,516]{1,0,2:T(2,128)} %copy.22) | data formatting | bytes 5812224 | tf_op jit(solution)/shard_map/convert_element_type | solution.py:102
  41.1 2.4 multiply_reduce_fusion
  43.5 0.5 copy-done.1
  44.0 1.2 fusion.7
  45.3 3.0 %fusion.16 = f32[512,704]{0,1:T(8,128)S(1)} fusion(bf16[5,1408,704]{1,2,0:T(8,128)(2,1)} %param.11, bf16[516,1408]{1,0:T(8,128)(2,1)S(1)} %fusion.7), kind=kOutput, calls=%fused_computation.22 | convolution fusion | flops 1015021568 | bytes 4866048 | tf_op jit(solution)/shard_map/dot_general | solution.py:106
  48.3 1.4 copy-done.4
  49.7 1.3 fusion.12
  51.0 1.3 fusion.10
  52.4 1.3 fusion.8
  53.7 1.5 add_add_fusion
  55.2 1.6 copy.23
  56.9 1.8 reshape.56
  58.6 0.9 reduce_sum.46
  59.6 27.1 %all-gather.6.cloned.1.call-done = bf16[704,1536]{0,1:T(8,128)(2,1)} async-done(((bf16[704,192]{0,1:T(8,128)(2,1)}), bf16[704,1536]{0,1:T(8,128)(2,1)}) %all-gather.6.cloned.1.call-update) | async-done | bytes 2162704 | tf_op jit(solution)/shard_map/all_gather | solution.py:112
  86.7 3.3 %convolution_convert_fusion.1 = bf16[128,1536]{1,0:T(8,128)(2,1)} fusion(bf16[704,1536]{0,1:T(8,128)(2,1)} %all-gather.6.cloned.1.call-done, f32[128,704]{1,0:T(8,128)S(1)} %reduce_sum.46), kind=kOutput, calls=%fused_computation.11 | convolution fusion | flops 277200896 | bytes 2916352 | tf_op jit(solution)/shard_map/dot_general | solution.py:115
  90.0 0.0 reduce-scatter.3.cloned.1.call-update
  90.0 0.0 all-gather.8.cloned.1.call-start
  90.1 0.1 fusion.44
  90.2 1.6 collective-permute-start.3
  91.8 0.8 constant_dynamic-slice_fusion
  92.6 0.0 reduce-scatter.5.cloned.1.call-start
  92.6 7.2 %collective-permute-done.3 = bf16[2,192,512]{2,1,0:T(8,128)(2,1)S(1)} collective-permute-done((bf16[2,192,512]{2,1,0:T(8,128)(2,1)S(1)}, bf16[2,192,512]{2,1,0:T(8,128)(2,1)S(1)}, u32[]{:S(2)}, u32[]{:S(2)}) %collective-permute-start.3) | collective-permute-done | bytes 393248 | tf_op jit(solution)/shard_map/ppermute | solution.py:23
  99.8 0.1 pad_maximum_fusion.1
  99.9 0.1 reverse_select_fusion.1
  100.0 2.6 collective-permute-start.4
  102.6 72.1 %all_gather.30 = bf16[1536,320]{1,0:T(8,128)(2,1)S(1)} all-gather(bf16[192,320]{1,0:T(8,128)(2,1)} %param.16), channel_id=1, replica_groups=mesh['grp'=2,'seq'=8,'col'=2] {'seq'}, dimensions={0}, use_global_device_ids=true | all-gather | bytes 1105920 | tf_op jit(solution)/shard_map/all_gather | solution.py:135
  174.7 0.1 pad_maximum_fusion
  174.9 0.3 reverse_select_fusion
  175.2 0.0 reduce-scatter.3.cloned.1.call-done
  175.2 1.1 fusion.39
  176.3 1.0 fusion.41
  177.4 2.1 all_gather.29
  179.5 0.5 convolution_convert_fusion.2
  180.0 0.4 fusion.35
  180.4 0.1 reshape.59
  180.5 26.8 %all_gather.31 = bf16[1024,128]{0,1:T(8,128)(2,1)S(1)} all-gather(bf16[128,128]{0,1:T(8,128)(2,1)S(1)} %slice.71), channel_id=1, replica_groups=mesh['grp'=2,'seq'=8,'col'=2] {'seq'}, dimensions={0}, use_global_device_ids=true | all-gather | bytes 294912 | tf_op jit(solution)/shard_map/all_gather | solution.py:144
  207.4 27.3 %all_gather.32 = bf16[1024,192]{0,1:T(8,128)(2,1)S(1)} all-gather(bf16[128,192]{0,1:T(8,128)(2,1)S(1)} %slice.72), channel_id=1, replica_groups=mesh['grp'=2,'seq'=8,'col'=2] {'seq'}, dimensions={0}, use_global_device_ids=true | all-gather | bytes 442368 | tf_op jit(solution)/shard_map/all_gather | solution.py:145
  234.7 0.5 fusion.59
  235.2 0.5 fusion.23
  235.7 0.6 fusion.34
  236.3 0.1 copy.24
  236.4 0.3 reshape.60
  236.7 0.0 all-gather.8.cloned.1.call-done
  236.7 3.4 %convolution_convert_fusion = bf16[128,1536]{1,0:T(8,128)(2,1)} fusion(bf16[128,768]{1,0:T(8,128)(2,1)S(1)} %reshape.60, bf16[768,1536]{0,1:T(8,128)(2,1)} %all-gather.8.cloned.1.call-done), kind=kOutput, calls=%fused_computation.10 | convolution fusion | flops 302186496 | bytes 2949120 | tf_op jit(solution)/shard_map/dot_general | solution.py:153
  240.1 5.1 %reduce-scatter.5.cloned.1.call-done = bf16[64,1536]{1,0:T(8,128)(2,1)} async-done(((bf16[128,1536]{1,0:T(8,128)(2,1)}), bf16[64,1536]{1,0:T(8,128)(2,1)}) %reduce-scatter.5.cloned.1.call-update) | async-done | bytes 196624 | tf_op jit(solution)/shard_map/reduce_scatter | solution.py:158
  245.2 1.7 convert_reduce_fusion
  246.9 0.2 fusion.36
  247.1 1.8 all-gather.1
  249.0 26.4 %all_gather.35 = bf16[64,128]{1,0:T(8,128)(2,1)S(1)} all-gather(bf16[8,128]{1,0:T(8,128)(2,1)S(1)} %get-tuple-element.11), channel_id=1, replica_groups=mesh['grp'=2,'seq'=8,'col'=2] {'seq'}, dimensions={0}, use_global_device_ids=true | all-gather | bytes 18432 | tf_op jit(solution)/shard_map/all_gather | solution.py:170
  275.4 0.1 fusion.53
  275.5 0.8 convolution_convert_fusion.3
  (35 shorter events, 0.2 us)
Async XLA Ops:
  7.2 239.7 %copy-start = (bf16[1536,256]{1,0:T(8,128)(2,1)S(1)}, bf16[1536,256]{1,0:T(8,128)(2,1)}, u32[]{:S(2)}) copy-start(bf16[1536,256]{1,0:T(8,128)(2,1)} %param.18) | copy-start | bytes 2359300
  7.2 24.3 %all-gather.10.cloned.1.call-start = ((), (), s32[]{:S(2)}) async-start(), calls=%async_computation.6 | async-start | bytes 2396160 | tf_op jit(solution)/shard_map/all_gather | solution.py:100
  8.7 12.5 %copy-start.6 = (bf16[192,1024]{1,0:T(8,128)(2,1)S(1)}, bf16[192,1024]{1,0:T(8,128)(2,1)}, u32[]{:S(2)}) copy-start(bf16[192,1024]{1,0:T(8,128)(2,1)} %param.15) | copy-start | bytes 1179652
  8.7 6.3 %collective-permute-start = (bf16[2,704]{1,0:T(2,128)(2,1)S(1)}, bf16[2,704]{1,0:T(2,128)(2,1)S(1)}, u32[]{:S(2)}, u32[]{:S(2)}) collective-permute-start(bf16[2,704]{1,0:T(2,128)(2,1)S(1)} %get-tuple-element.4), channel_id=1, source_target_pairs={{0,2},{2,4},{4,6},{6,8},{8,10},{10,12},{12,14},{1,3},{3,5},{5,7},{... | collective-permute-start | bytes 8456 | tf_op jit(solution)/shard_map/ppermute | solution.py:41
  13.7 5.5 %collective-permute-start.1 = (bf16[2,704]{1,0:T(2,128)(2,1)S(1)}, bf16[2,704]{1,0:T(2,128)(2,1)S(1)}, u32[]{:S(2)}, u32[]{:S(2)}) collective-permute-start(bf16[2,704]{1,0:T(2,128)(2,1)S(1)} %get-tuple-element.5), channel_id=1, source_target_pairs={{2,0},{4,2},{6,4},{8,6},{10,8},{12,10},{14,12},{3,1},{5,3},{7,5},{... | collective-permute-start | bytes 8456 | tf_op jit(solution)/shard_map/ppermute | solution.py:42
  20.4 66.3 %all-gather.6.cloned.1.call-start = ((), (), s32[]{:S(2)}) async-start(), calls=%async_computation.2 | async-start | bytes 2654208 | tf_op jit(solution)/shard_map/all_gather | solution.py:112
  21.1 154.1 %reduce-scatter.3.cloned.1.call-start = ((), (), s32[]{:S(2)}) async-start(), calls=%async_computation.3 | async-start | bytes 589824 | tf_op jit(solution)/shard_map/reduce_scatter | solution.py:114
  21.2 68.9 %collective-permute-start.2 = (bf16[1,192,512]{2,1,0:T(8,128)(2,1)S(1)}, bf16[1,192,512]{2,1,0:T(8,128)(2,1)S(1)}, u32[]{:S(2)}, u32[]{:S(2)}) collective-permute-start(bf16[1,192,512]{2,1,0:T(8,128)(2,1)S(1)} %get-tuple-element.9), channel_id=1, source_target_pairs={{0,2},{2,0},{4,6},{6,4},{8,10},{10,8},{12,14},{14,12},{1,3},{3,1},... | collective-permute-start | bytes 589832 | tf_op jit(solution)/shard_map/ppermute | solution.py:23
  41.1 2.9 %copy-start.1 = (f32[1408,516]{0,1:T(8,128)S(1)}, f32[1408,516]{0,1:T(8,128)}, u32[]{:S(2)}) copy-start(f32[1408,516]{0,1:T(8,128)} %reshape.70) | copy-start | bytes 8718340
  41.1 2.9 %copy-start.8 = (f32[1408]{0:T(1024)S(1)}, f32[1408]{0:T(1024)}, u32[]{:S(2)}) copy-start(f32[1408]{0:T(1024)} %param.12) | copy-start | bytes 16900
  45.3 4.4 %copy-start.4 = (bf16[5,1408,704]{1,2,0:T(8,128)(2,1)S(1)}, bf16[5,1408,704]{1,2,0:T(8,128)(2,1)}, u32[]{:S(2)}) copy-start(bf16[5,1408,704]{1,2,0:T(8,128)(2,1)} %param.11) | copy-start | bytes 29736964
  52.4 1.4 copy-start.2
  90.0 1.8 copy-start.5
  90.0 146.7 %all-gather.8.cloned.1.call-start = ((), (), s32[]{:S(2)}) async-start(), calls=%async_computation.4 | async-start | bytes 2654208 | tf_op jit(solution)/shard_map/all_gather | solution.py:155
  90.2 9.5 %collective-permute-start.3 = (bf16[2,192,512]{2,1,0:T(8,128)(2,1)S(1)}, bf16[2,192,512]{2,1,0:T(8,128)(2,1)S(1)}, u32[]{:S(2)}, u32[]{:S(2)}) collective-permute-start(bf16[2,192,512]{2,1,0:T(8,128)(2,1)S(1)} %get-tuple-element.7), channel_id=1, source_target_pairs={{0,4},{2,6},{4,0},{6,2},{8,12},{10,14},{12,8},{14,10},{1,5},{3,7},... | collective-permute-start | bytes 1179656 | tf_op jit(solution)/shard_map/ppermute | solution.py:23
  92.6 152.7 %reduce-scatter.5.cloned.1.call-start = ((), (), s32[]{:S(2)}) async-start(), calls=%async_computation.5 | async-start | bytes 589824 | tf_op jit(solution)/shard_map/reduce_scatter | solution.py:158
  100.0 74.7 %collective-permute-start.4 = (bf16[4,192,512]{2,1,0:T(8,128)(2,1)S(1)}, bf16[4,192,512]{2,1,0:T(8,128)(2,1)S(1)}, u32[]{:S(2)}, u32[]{:S(2)}) collective-permute-start(bf16[4,192,512]{2,1,0:T(8,128)(2,1)S(1)} %bitcast.61), channel_id=1, source_target_pairs={{0,8},{2,10},{4,12},{6,14},{8,0},{10,2},{12,4},{14,6},{1,9},{3,11}... | collective-permute-start | bytes 2359304 | tf_op jit(solution)/shard_map/ppermute | solution.py:23
  174.9 1.5 copy-start.9
  236.7 8.5 %copy-start.3 = (bf16[64,1536]{1,0:T(8,128)(2,1)S(1)}, bf16[64,1536]{1,0:T(8,128)(2,1)}, u32[]{:S(2)}) copy-start(bf16[64,1536]{1,0:T(8,128)(2,1)} %reduce-scatter.3.cloned.1.call-done) | copy-start | bytes 589828
  240.1 35.3 %copy-start.7 = (bf16[128,128]{1,0:T(8,128)(2,1)S(1)}, bf16[128,128]{1,0:T(8,128)(2,1)}, u32[]{:S(2)}) copy-start(bf16[128,128]{1,0:T(8,128)(2,1)} %param.19) | copy-start | bytes 98308
Sparse Core Ops, SparseCore 0:
  20.5 10.9 all-gather.9
  33.7 52.9 all-gather.5
  90.2 6.3 reduce-scatter.2
  98.6 84.9 all-gather.7
  240.2 4.9 reduce-scatter.4
